TPU v7x, 256 devices: a whole 4x4x8 slice. The times are simulated.
256 devices in a mesh: sub: 16 (over z, core), root: 16 (over y, x).
Axes of the slice: x: 4, y: 4, z: 8, core: 2. Of those that a mesh axis runs over, the one named last changes fastest.
Arguments:
- right_side: bfloat16 [16, 32768, 256], P('root', 'sub'), may hold values from -6 to 6
- leaf_inverse: bfloat16 [16, 32768, 512], P('root', 'sub'), may hold values from -0.25 to 0.25
- leaf_basis: bfloat16 [16, 32768, 256], P('root', 'sub'), may hold values from -0.25 to 0.25
- local_merge: bfloat16 [16, 24576, 512], P('root', 'sub'), may hold values from -0.25 to 0.25
- local_transfer: bfloat16 [16, 24576, 256], P('root', 'sub'), may hold values from -0.25 to 0.25
- upper_merge: bfloat16 [16, 7680, 512], P('root', 'sub'), may hold values from -0.25 to 0.25
- upper_transfer: bfloat16 [16, 7680, 256], P('root', 'sub'), may hold values from -0.25 to 0.25
- top_inverse: bfloat16 [4096, 4096], P('root', 'sub'), may hold values from -0.09375 to 0.09375
Outputs:
- solution: float32 [16, 32768, 256], P('root', 'sub')
All inputs are finite; a program needn't handle non-finite values.
Results may differ from a plain program's by a relative error of at most 0.02.
Values may be sent and summed in bfloat16 or wider, within the bound.
A program may use at most 128 MiB of HBM per device.

v0:
```python
import jax
import jax.numpy as jnp
from jax import lax
from jax.sharding import Mesh
from jax.sharding import PartitionSpec as P

SUB = ("sub_0", "sub_1")


def side_by_side(arrays, axis, dim, along):
    widths = [a.shape[along] for a in arrays]
    both = jnp.concatenate(arrays, axis=along)
    filled = lax.all_gather(both, axis, axis=dim, tiled=True)
    return tuple(jnp.split(filled, [sum(widths[:k]) for k in range(1, len(widths))], axis=along))


def in_order(blocks, dim):
    shape = list(blocks.shape[1:])
    shape[dim] *= blocks.shape[0]
    return jnp.moveaxis(blocks, 0, dim).reshape(shape)


def from_everyone(shard, axis):
    length = lax.axis_size(axis)
    return lax.all_to_all(
        jnp.broadcast_to(shard[None], (length, *shard.shape)), axis, 0, 0, tiled=True
    )


def collect(shard, axis, dim):
    return in_order(from_everyone(shard, axis), dim)


def whole_of(shard, axes, dim):
    if not axes:
        return shard
    nearer = lax.all_gather(shard, axes[-1], axis=dim, tiled=True)
    return whole_of(nearer, axes[:-1], dim)


def batch_product(left, right):
    return jnp.einsum("nij,njk->nik", left, right, preferred_element_type=jnp.float32)


def batch_transposed(left, right):
    return jnp.einsum("nji,njk->nik", left, right, preferred_element_type=jnp.float32)


def merge_up(coeffs, merge_mat, transfer):
    paired = coeffs.astype(jnp.bfloat16).reshape(
        merge_mat.shape[0], merge_mat.shape[1], coeffs.shape[-1]
    )
    inner_part = batch_product(merge_mat, paired)
    return (inner_part, batch_transposed(transfer, inner_part.astype(jnp.bfloat16)))


def merge_down(parent, inner_part, merge_mat, transfer):
    lifted = batch_product(transfer, parent.astype(jnp.bfloat16)).astype(jnp.bfloat16)
    children = inner_part - batch_product(merge_mat, lifted)
    return children.reshape(-1, transfer.shape[2], children.shape[-1])


def body(
    right_side,
    leaf_inverse,
    leaf_basis,
    local_merge,
    local_transfer,
    upper_merge,
    upper_transfer,
    top_inverse,
):
    leaf_size = leaf_inverse.shape[2]
    rank_size = leaf_basis.shape[2]
    columns = right_side.shape[2]
    double = 2 * rank_size
    leaf_count = right_side.shape[1] // leaf_size
    leaf_depth = leaf_count.bit_length() - 1
    sub_count = lax.axis_size(SUB)
    sub_depth = sub_count.bit_length() - 1
    position = lax.axis_index(SUB)
    leaf_inv = leaf_inverse.reshape(leaf_count, leaf_size, leaf_size)
    basis_block = leaf_basis.reshape(leaf_count, leaf_size, rank_size)
    local_m = local_merge.reshape(leaf_count - 1, double, double)
    local_w = local_transfer.reshape(leaf_count - 1, double, rank_size)
    solved = batch_product(leaf_inv, right_side.reshape(leaf_count, leaf_size, columns))
    coeffs = batch_transposed(basis_block, solved.astype(jnp.bfloat16))
    inner_saved = []
    for tier_no in range(1, leaf_depth + 1):
        node_count = leaf_count >> tier_no
        start = leaf_count - 2 * node_count
        inner_part, coeffs = merge_up(
            coeffs, local_m[start : start + node_count], local_w[start : start + node_count]
        )
        inner_saved.append(inner_part)
    upper_saved = []
    all_rows, all_cols = side_by_side((upper_merge, upper_transfer), SUB, 1, 2)
    roots = lax.all_gather(coeffs[0].astype(jnp.bfloat16), SUB, axis=0, tiled=True)
    all_rows = all_rows[0].reshape(sub_count, -1, double)
    all_cols = all_cols[0].reshape(sub_count, -1, rank_size)
    current = roots.reshape(sub_count, rank_size, columns)
    level_mats = []
    for tier_no in range(1, sub_depth + 1):
        height = double >> tier_no
        offset = double - 2 * height
        merge_mat = all_rows[:, offset : offset + height].reshape(
            sub_count >> tier_no, double, double
        )
        transfer = all_cols[:, offset : offset + height].reshape(
            sub_count >> tier_no, double, rank_size
        )
        inner_part, current = merge_up(current, merge_mat, transfer)
        upper_saved.append(inner_part)
        level_mats.append((merge_mat, transfer))
    root_coeff = current[0]
    stacked = collect(root_coeff.astype(jnp.bfloat16), "root", 0)
    full_rows = whole_of(top_inverse, SUB, 1)
    coupling = jnp.dot(full_rows, stacked, preferred_element_type=jnp.float32)
    parent = coupling[None]
    for tier_no in range(sub_depth, 0, -1):
        merge_mat, transfer = level_mats[tier_no - 1]
        parent = merge_down(parent, upper_saved[tier_no - 1], merge_mat, transfer)
    parent = lax.dynamic_slice_in_dim(parent, position, 1, 0)
    for tier_no in range(leaf_depth, 0, -1):
        node_count = leaf_count >> tier_no
        start = leaf_count - 2 * node_count
        parent = merge_down(
            parent,
            inner_saved[tier_no - 1],
            local_m[start : start + node_count],
            local_w[start : start + node_count],
        )
    spread = batch_product(basis_block, parent.astype(jnp.bfloat16)).astype(jnp.bfloat16)
    result = solved - batch_product(leaf_inv, spread)
    return result.reshape(1, leaf_count * leaf_size, columns)


def solution(mesh):
    finer = Mesh(mesh.devices.reshape(8, 2, mesh.shape["root"]), ("sub_0", "sub_1", "root"))
    placed = (
        P("root", SUB, None),
        P("root", SUB, None),
        P("root", SUB, None),
        P("root", SUB, None),
        P("root", SUB, None),
        P("root", SUB, None),
        P("root", SUB, None),
        P("root", SUB),
    )
    return jax.shard_map(
        body, mesh=finer, in_specs=placed, out_specs=P("root", SUB, None), check_vma=False
    )
```

profile of v0, /device:TPU:1, one launch (start us, length us, event | category | flops | bytes accessed | tf_op | source)
XLA Modules:
  0.0 241.1 jit_solution(11442803951525167674)
XLA Ops:
  6.5 0.0 all-gather.6.cloned.1.call-start
  6.5 1.2 slice.50
  7.8 1.5 slice.48
  9.3 0.0 copy-start.17
  9.3 0.7 fusion.40
  10.0 0.0 copy-start.6
  10.0 0.9 copy-done.17
  10.9 0.5 convolution_convert_fusion.5
  11.4 0.0 copy-done.8
  11.4 0.5 fusion.41
  12.0 0.0 copy-done.6
  12.0 0.0 copy-done.14
  12.0 0.0 copy-start.19
  12.0 0.4 convolution_convert_fusion.9
  12.4 0.0 copy-start.20
  12.4 1.4 fusion.17
  13.8 0.8 copy-done.12
  14.6 1.8 fusion.13
  16.4 0.0 all-gather.6.cloned.1.call-update
  16.5 0.0 all-gather.4.cloned.1.call-start
  16.5 2.0 pad_maximum_fusion
  18.5 0.0 all-gather.4.cloned.1.call-update
  18.5 0.0 all-gather.8.cloned.1.call-start
  18.6 5.0 %all_gather.14 = bf16[256,512]{1,0:T(8,128)(2,1)} all-gather(bf16[256,256]{1,0:T(8,128)(2,1)S(1)} %copy-done.20), channel_id=1, replica_groups=mesh['sub_0'=8,'sub_1'=2,'root'=16] {'sub_1'}, dimensions={1}, use_global_device_ids=true | all-gather | bytes 393216 | tf_op jit(solution)/shard_map/all_gather | solution.py:37
  23.5 0.0 all-gather.8.cloned.1.call-update
  23.6 37.9 %all-gather.6.cloned.1.call-done = bf16[4096,256]{0,1:T(8,128)(2,1)} async-done(((bf16[256,256]{0,1:T(8,128)(2,1)}), bf16[4096,256]{0,1:T(8,128)(2,1)}) %all-gather.6.cloned.1.call-update) | async-done | bytes 2097168 | tf_op jit(solution)/shard_map/all_gather | solution.py:98
  61.4 4.1 %copy.30 = bf16[4096,256]{1,0:T(8,128)(2,1)} copy(bf16[4096,256]{0,1:T(8,128)(2,1)} %all-gather.6.cloned.1.call-done) | data formatting | bytes 4194304 | tf_op jit(solution)/shard_map/reshape;reshape | solution.py:50
  65.5 68.7 %all-gather.4.cloned.1.call-done = bf16[1,7680,768]{2,1,0:T(8,128)(2,1)} async-done(((bf16[1,480,768]{2,1,0:T(8,128)(2,1)}), bf16[1,7680,768]{2,1,0:T(8,128)(2,1)}) %all-gather.4.cloned.1.call-update) | async-done | bytes 11796496 | tf_op jit(solution)/shard_map/all_gather | solution.py:13
  134.3 2.4 %split.9 = bf16[1,7680,256]{2,1,0:T(8,128)(2,1)S(1)} slice(bf16[1,7680,768]{2,1,0:T(8,128)(2,1)} %all-gather.4.cloned.1.call-done), slice={[0:1], [0:7680], [512:768]} | slice | bytes 7864320 | tf_op jit(solution)/shard_map/split | solution.py:14
  136.7 0.8 slice.67
  137.6 0.1 slice.65
  137.7 0.1 slice.63
  137.8 7.8 %split.8 = bf16[1,7680,512]{2,1,0:T(8,128)(2,1)} slice(bf16[1,7680,768]{2,1,0:T(8,128)(2,1)} %all-gather.4.cloned.1.call-done), slice={[0:1], [0:7680], [0:512]} | slice | bytes 15728640 | tf_op jit(solution)/shard_map/split | solution.py:14
  145.6 1.1 slice.68
  146.7 1.5 slice.66
  148.2 2.2 slice.64
  150.4 3.5 %slice.62 = bf16[16,256,512]{2,1,0:T(8,128)(2,1)S(1)} slice(bf16[16,480,512]{2,1,0:T(8,128)(2,1)} %bitcast.104), slice={[0:16], [0:256], [0:512]} | slice | bytes 8388608 | tf_op jit(solution)/shard_map/slice | solution.py:106
  153.8 0.2 copy-done.11
  154.0 1.3 fusion.42
  155.3 0.5 copy-done.2
  155.8 0.9 fusion.5
  156.8 1.1 copy-done.1
  157.8 0.7 fusion.43
  158.6 0.5 convolution_convert_fusion.4
  159.1 0.4 fusion.44
  159.6 0.3 copy-done.3
  159.9 1.0 copy-done.7
  160.9 0.4 convolution_convert_fusion.8
  161.3 0.3 fusion.45
  161.6 0.8 copy-done.13
  162.4 0.3 convolution_convert_fusion.10
  162.7 1.5 broadcast_in_dim.2
  164.2 6.6 %all-to-all-start = ((bf16[16,256,256]{2,1,0:T(8,128)(2,1)}), bf16[16,256,256]{2,1,0:T(8,128)(2,1)}, u32[]{:S(2)}, u32[]{:S(2)}) async-start(bf16[16,256,256]{2,1,0:T(8,128)(2,1)} %broadcast_in_dim.2), calls=%async_computation | async-start | bytes 4194304 | tf_op jit(solution)/shard_map/all_to_all | solution.py:25
  170.8 0.1 all-gather.8.cloned.1.call-done
  170.9 32.6 %all-to-all-done = bf16[16,256,256]{2,1,0:T(8,128)(2,1)} async-done(((bf16[16,256,256]{2,1,0:T(8,128)(2,1)}), bf16[16,256,256]{2,1,0:T(8,128)(2,1)}, u32[]{:S(2)}, u32[]{:S(2)}) %all-to-all-start) | async-done | bytes 2097184 | tf_op jit(solution)/shard_map/all_to_all | solution.py:25
  203.5 3.0 %convolution_convert_fusion.12 = bf16[256,256]{1,0:T(8,128)(2,1)S(1)} fusion(bf16[4096,256]{1,0:T(8,128)(2,1)} %bitcast.26, bf16[256,4096]{1,0:T(8,128)(2,1)} %all-gather.8.cloned.1.call-done), kind=kOutput, calls=%fused_computation.29 | convolution fusion | flops 536936448 | bytes 4325376 | tf_op jit(solution)/shard_map/dot_general | solution.py:118
  206.5 2.5 %fusion.11 = bf16[512,256]{1,0:T(8,128)(2,1)} fusion(f32[512,256]{1,0:T(8,128)} %copy-done.13, bf16[512,512]{1,0:T(8,128)(2,1)} %bitcast.125, bf16[512,256]{1,0:T(8,128)(2,1)S(1)} %bitcast.132, bf16[256,256]{1,0:T(8,128)(2,1)S(1)} %convolution_convert_fusion.12), kind=kOutput, calls=%fused_computation.21 | convolution fusion | flops 201719808 | bytes 1703936 | tf_op jit(solution)/shard_map/nij,njk->nik/dot_general | solution.py:42
  209.0 3.2 %fusion.8 = bf16[2,512,256]{2,1,0:T(8,128)(2,1)} fusion(f32[2,512,256]{2,1,0:T(8,128)} %copy-done.7, bf16[2,512,512]{2,1,0:T(8,128)(2,1)} %bitcast.118, bf16[2,512,256]{2,1,0:T(8,128)(2,1)} %bitcast.122, bf16[2,256,256]{2,1,0:T(8,128)(2,1)} %bitcast.141), kind=kOutput, calls=%fused_computation.12 | convolution fusion | flops 403439616 | bytes 3407872 | tf_op jit(solution)/shard_map/nij,njk->nik/dot_general | solution.py:42
  212.3 4.7 %subtract_convert_fusion = bf16[4,512,256]{2,1,0:T(8,128)(2,1)} fusion(f32[4,512,256]{2,1,0:T(8,128)} %copy-done.3, bf16[4,512,512]{2,1,0:T(8,128)(2,1)} %bitcast.108, bf16[4,512,256]{2,1,0:T(8,128)(2,1)} %bitcast.116, bf16[4,256,256]{2,1,0:T(8,128)(2,1)} %bitcast.135), kind=kOutput, calls=%fused_computation.3 | convolution fusion | flops 806879232 | bytes 6815744 | tf_op jit(solution)/shard_map/nij,njk->nik/dot_general | solution.py:42
  217.0 7.5 %convolution_subtract_fusion = bf16[8,512,256]{2,1,0:T(8,128)(2,1)} fusion(f32[8,512,256]{2,1,0:T(8,128)} %copy-done.1, bf16[8,512,512]{2,1,0:T(8,128)(2,1)} %bitcast.100, bf16[8,512,256]{2,1,0:T(8,128)(2,1)} %bitcast.106, bf16[8,256,256]{2,1,0:T(8,128)(2,1)} %bitcast.129), kind=kOutput, calls=%fused_computation | convolution fusion | flops 1613758464 | bytes 13631488 | tf_op jit(solution)/shard_map/nij,njk->nik/dot_general | solution.py:42
  224.5 1.8 fusion.12
  226.3 2.8 %fusion.10 = bf16[2,512,256]{1,2,0:T(8,128)(2,1)} fusion(f32[2,256,512]{2,1,0:T(8,128)S(1)} %fusion.41, bf16[2,512,512]{2,1,0:T(8,128)(2,1)} %bitcast.114, bf16[2,512,256]{2,1,0:T(8,128)(2,1)} %bitcast.121, bf16[32,2,8,256]{3,2,1,0:T(8,128)(2,1)S(1)} %bitcast.140), kind=kOutput, calls=%fused_computation.18 | convolution fusion | flops 403439616 | bytes 3407872 | tf_op jit(solution)/shard_map/nij,njk->nik/dot_general | solution.py:42
  229.1 1.2 copy.20
  230.3 4.3 %bitcast_subtract_fusion = f32[4,512,256]{2,1,0:T(8,128)} fusion(f32[4,512,256]{2,1,0:T(8,128)} %copy-done.6, bf16[4,512,512]{2,1,0:T(8,128)(2,1)S(1)} %bitcast.98, bf16[4,256,256]{2,1,0:T(8,128)(2,1)S(1)} %bitcast.136, bf16[4,512,256]{2,1,0:T(8,128)(2,1)} %bitcast.126), kind=kOutput, calls=%fused_computation.1 | convolution fusion | flops 806354944 | bytes 7864320 | tf_op jit(solution)/shard_map/nij,njk->nik/dot_general | solution.py:42
  (28 shorter events, 0.1 us)
Async XLA Ops:
  6.5 2.7 %copy-start = (bf16[1,2048,512]{2,1,0:T(8,128)(2,1)S(1)}, bf16[1,2048,512]{2,1,0:T(8,128)(2,1)}, u32[]{:S(2)}) copy-start(bf16[1,2048,512]{2,1,0:T(8,128)(2,1)} %param.9) | copy-start | bytes 6291460
  6.5 2.8 %copy-start.18 = (bf16[1,2048,256]{2,1,0:T(8,128)(2,1)S(1)}, bf16[1,2048,256]{2,1,0:T(8,128)(2,1)}, u32[]{:S(2)}) copy-start(bf16[1,2048,256]{2,1,0:T(8,128)(2,1)} %param.8) | copy-start | bytes 3145732
  6.5 54.9 %all-gather.6.cloned.1.call-start = ((), (), s32[]{:S(2)}) async-start(), calls=%async_computation.2 | async-start | bytes 2228224 | tf_op jit(solution)/shard_map/all_gather | solution.py:98
  7.8 4.2 %copy-start.14 = (bf16[1,1024,256]{2,1,0:T(8,128)(2,1)}, bf16[1,1024,256]{2,1,0:T(8,128)(2,1)S(1)}, u32[]{:S(2)}) copy-start(bf16[1,1024,256]{2,1,0:T(8,128)(2,1)S(1)} %slice.50) | copy-start | bytes 1572868
  9.3 2.2 copy-start.8
  9.3 1.6 copy-start.17
  10.0 1.9 copy-start.6
  12.0 4.5 %copy-start.19 = (bf16[1,480,256]{2,1,0:T(8,128)(2,1)S(1)}, bf16[1,480,256]{2,1,0:T(8,128)(2,1)}, u32[]{:S(2)}) copy-start(bf16[1,480,256]{2,1,0:T(8,128)(2,1)} %param.14) | copy-start | bytes 737284
  12.4 6.2 %copy-start.20 = (bf16[256,256]{1,0:T(8,128)(2,1)S(1)}, bf16[256,256]{1,0:T(8,128)(2,1)}, u32[]{:S(2)}) copy-start(bf16[256,256]{1,0:T(8,128)(2,1)} %param.15) | copy-start | bytes 393220
  13.8 0.8 copy-start.12
  16.5 117.8 %all-gather.4.cloned.1.call-start = ((), (), s32[]{:S(2)}) async-start(), calls=%async_computation.1 | async-start | bytes 12533760 | tf_op jit(solution)/shard_map/all_gather | solution.py:13
  18.5 152.4 %all-gather.8.cloned.1.call-start = ((), (), s32[]{:S(2)}) async-start(), calls=%async_computation.3 | async-start | bytes 2359296 | tf_op jit(solution)/shard_map/all_gather | solution.py:37
  137.6 20.9 %copy-start.9 = (bf16[16,128,256]{2,1,0:T(8,128)(2,1)}, bf16[16,128,256]{2,1,0:T(8,128)(2,1)S(1)}, u32[]{:S(2)}) copy-start(bf16[16,128,256]{2,1,0:T(8,128)(2,1)S(1)} %slice.65) | copy-start | bytes 3145732
  137.8 18.0 %copy-start.4 = (bf16[16,256,256]{2,1,0:T(8,128)(2,1)}, bf16[16,256,256]{2,1,0:T(8,128)(2,1)S(1)}, u32[]{:S(2)}) copy-start(bf16[16,256,256]{2,1,0:T(8,128)(2,1)S(1)} %slice.63) | copy-start | bytes 6291460
  146.7 14.6 %copy-start.16 = (bf16[16,32,512]{2,1,0:T(8,128)(2,1)}, bf16[16,32,512]{2,1,0:T(8,128)(2,1)S(1)}, u32[]{:S(2)}) copy-start(bf16[16,32,512]{2,1,0:T(8,128)(2,1)S(1)} %slice.68) | copy-start | bytes 1572868
  148.2 10.9 %copy-start.10 = (bf16[16,64,512]{2,1,0:T(8,128)(2,1)}, bf16[16,64,512]{2,1,0:T(8,128)(2,1)S(1)}, u32[]{:S(2)}) copy-start(bf16[16,64,512]{2,1,0:T(8,128)(2,1)S(1)} %slice.66) | copy-start | bytes 3145732
  150.4 7.5 %copy-start.5 = (bf16[16,128,512]{2,1,0:T(8,128)(2,1)}, bf16[16,128,512]{2,1,0:T(8,128)(2,1)S(1)}, u32[]{:S(2)}) copy-start(bf16[16,128,512]{2,1,0:T(8,128)(2,1)S(1)} %slice.64) | copy-start | bytes 6291460
  150.4 3.7 %copy-start.11 = (bf16[4096,256]{1,0:T(8,128)(2,1)S(1)}, bf16[4096,256]{1,0:T(8,128)(2,1)}, u32[]{:S(2)}) copy-start(bf16[4096,256]{1,0:T(8,128)(2,1)} %copy.30) | copy-start | bytes 6291460
  153.8 2.0 copy-start.2
  155.8 2.0 copy-start.1
  158.5 1.4 copy-start.3
  159.1 1.8 copy-start.15
  159.9 1.0 copy-start.7
  161.6 0.8 copy-start.13
  164.2 39.3 %all-to-all-start = ((bf16[16,256,256]{2,1,0:T(8,128)(2,1)}), bf16[16,256,256]{2,1,0:T(8,128)(2,1)}, u32[]{:S(2)}, u32[]{:S(2)}) async-start(bf16[16,256,256]{2,1,0:T(8,128)(2,1)} %broadcast_in_dim.2), calls=%async_computation | async-start | bytes 4194304 | tf_op jit(solution)/shard_map/all_to_all | solution.py:25
Sparse Core Ops, SparseCore 0:
  16.6 44.7 all-gather.5
  63.3 70.9 all-gather.3
  136.1 34.8 all-gather.7
where the time goes:
time: 242 us; the launch traced here: 241 us
  waiting for transfers between devices  139 us (57%)
  matrix products  40 us (17%)
  local copies, waits for them, and re-layouts  34.7 us (14%)
  between operations  13.5 us (6%)
  starting transfers between devices  6.68 us (3%)
  blocking collectives  4.96 us (2%)
    all_gather x1, waiting for transfers between devices, side_by_side(): filled = lax.all_gather(both, axis, axis=dim, tiled=True)  68.7 us
    all_gather x1, waiting for transfers between devices, body(): lax.all_gather(coeffs[0].astype(jnp.bfloat16), SUB, axis=0, tiled=True)  37.9 us
    all_to_all x1, waiting for transfers between devices, from_everyone(): lax.all_to_all(jnp.broadcast_to(shard[None], (length, *shard.shape)), axi...  32.6 us
    dot_general x14, matrix products, batch_product(): jnp.einsum('nij,njk->nik', left, right, preferred_element_type=jnp.float32)  32.2 us
    split x2, local copies, waits for them, and re-layouts, side_by_side(): jnp.split(filled, [sum(widths[:k]) for k in range(1, len(widths))], axis=...  10.2 us
    slice x4, local copies, waits for them, and re-layouts, body(): all_rows[:, offset:offset + height]  8.2 us
    all_to_all x1, starting transfers between devices, from_everyone(): lax.all_to_all(jnp.broadcast_to(shard[None], (length, *shard.shape)), axi...  6.6 us
    unnamed x42, local copies, waits for them, and re-layouts  5.68 us
  transfers between devices with their start and end apart: 4, of which 4 were waited for; matrix products, arithmetic and copies ran while one was open for 13% of the time, Pallas kernels for 0%

commit v1 on v0

v1 whole, which is shorter than its diff:
```python
import jax
import jax.numpy as jnp
from jax import lax
from jax.experimental import pallas as pl
from jax.experimental.pallas import tpu as pltpu
from jax.sharding import PartitionSpec as P

MESH = pl.DeviceIdType.MESH
BF = jnp.bfloat16
F32 = jnp.float32


def mul(a, b):
    return lax.dot_general(a, b, (((1,), (0,)), ((), ())), preferred_element_type=F32)


def mul_t(a, b):
    return lax.dot_general(a, b, (((1,), (1,)), ((), ())), preferred_element_type=F32)


def t_mul(a, b):
    return lax.dot_general(a, b, (((0,), (0,)), ((), ())), preferred_element_type=F32)


def kernel(
    b_hbm, d_hbm, u_hbm, lm_hbm, lw_hbm, um_hbm, uw_hbm, top_hbm,
    out_hbm,
    bv, dv, uv, lm, lw, m1, w1, m2, w2, rm, rw, tp,
    cl, cn, ct, p1, c1, p2, c2, p34, rt, t4,
    t2s, f2, t1s, f1, t0s, f0, gq, sv, hv,
    load_sem, own_sem, out_sem, send_sem, up_sem, ring_sem, small_sem, root_sem, t4_sem,
):
    s = lax.axis_index("sub")
    r = lax.axis_index("root")
    k = lax.rem(s, 2)
    z0 = lax.rem(s // 2, 2)
    g = s // 4
    slot = 8 * k + 4 * z0 + g
    partner = s + 1 - 2 * k
    across = s + 2 - 4 * z0
    right = lax.rem(s + 2, 16)
    left = lax.rem(s + 14, 16)

    barrier = pltpu.get_barrier_semaphore()
    for i in range(1, 16):
        pl.semaphore_signal(barrier, inc=1, device_id=(lax.rem(s + i, 16), r), device_id_type=MESH)
    for i in range(1, 16):
        pl.semaphore_signal(barrier, inc=1, device_id=(s, lax.rem(r + i, 16)), device_id_type=MESH)

    def load(i):
        rows = pl.ds(i * 512, 512)
        return [
            pltpu.make_async_copy(d_hbm.at[rows], dv.at[i], load_sem.at[0, i]),
            pltpu.make_async_copy(b_hbm.at[rows], bv.at[i], load_sem.at[1, i]),
            pltpu.make_async_copy(u_hbm.at[rows], uv.at[i], load_sem.at[2, i]),
        ]

    def load_local(i):
        rows = pl.ds(i * 512, 512)
        return [
            pltpu.make_async_copy(lm_hbm.at[rows], lm.at[i], load_sem.at[3, i]),
            pltpu.make_async_copy(lw_hbm.at[rows], lw.at[i], load_sem.at[4, i]),
        ]

    for i in range(4):
        for c in load(i):
            c.start()
    for i in range(3):
        for c in load_local(i):
            c.start()
    place1 = pl.ds(k * 256, 256)
    place2 = 2 * z0 + k
    here2 = pl.ds(place2 * 128, 128)
    first, second, third = pl.ds(0, 256), pl.ds(256, 128), pl.ds(384, 96)
    own = [
        pltpu.make_async_copy(um_hbm.at[first], m1.at[place1], own_sem.at[0]),
        pltpu.make_async_copy(uw_hbm.at[first], w1.at[place1], own_sem.at[1]),
        pltpu.make_async_copy(um_hbm.at[second], m2.at[here2], own_sem.at[2]),
        pltpu.make_async_copy(uw_hbm.at[second], w2.at[here2], own_sem.at[3]),
        pltpu.make_async_copy(um_hbm.at[third], rm.at[s], own_sem.at[4]),
        pltpu.make_async_copy(uw_hbm.at[third], rw.at[s], own_sem.at[5]),
        pltpu.make_async_copy(top_hbm, tp.at[s], own_sem.at[6]),
    ]
    for c in own:
        c.start()

    sent = []

    def send(src, dst, sem, to):
        copy = pltpu.make_async_remote_copy(
            src_ref=src, dst_ref=dst, send_sem=send_sem.at[len(sent)], recv_sem=sem,
            device_id=to, device_id_type=MESH,
        )
        copy.start()
        sent.append(copy)

    def arrived(dst, sem):
        pltpu.make_async_remote_copy(
            src_ref=dst, dst_ref=dst, send_sem=send_sem.at[0], recv_sem=sem,
            device_id=(partner, r), device_id_type=MESH,
        ).wait_recv()

    pl.semaphore_wait(barrier, 30)

    rings = ((um_hbm.at[third], rm), (uw_hbm.at[third], rw), (top_hbm, tp))

    def ring_own(a):
        src, dst = rings[a]
        send(src, dst.at[s], ring_sem.at[a, s], (right, r))
        send(src, dst.at[s], ring_sem.at[a, s], (left, r))
        send(src, dst.at[s], ring_sem.at[a, s], (partner, r))

    reach = ((4, 3), (3, 4), (3, 4))

    def relay(a, hop):
        dst = rings[a][1]
        if hop <= reach[a][0]:
            b = lax.rem(s + 16 - 2 * hop, 16)
            arrived(dst.at[b], ring_sem.at[a, b])
            if hop < reach[a][0]:
                send(dst.at[b], dst.at[b], ring_sem.at[a, b], (right, r))
            send(dst.at[b], dst.at[b], ring_sem.at[a, b], (partner, r))
        if hop <= reach[a][1]:
            b = lax.rem(s + 2 * hop, 16)
            arrived(dst.at[b], ring_sem.at[a, b])
            if hop < reach[a][1]:
                send(dst.at[b], dst.at[b], ring_sem.at[a, b], (left, r))
            send(dst.at[b], dst.at[b], ring_sem.at[a, b], (partner, r))

    def ring_rest(a):
        dst = rings[a][1]
        for i in range(8):
            b = lax.rem(partner + 2 * i, 16)
            arrived(dst.at[b], ring_sem.at[a, b])

    ring_own(0)
    ring_own(1)
    send(um_hbm.at[second], m2.at[here2], up_sem.at[0, place2], (across, r))
    send(uw_hbm.at[second], w2.at[here2], up_sem.at[1, place2], (across, r))
    send(um_hbm.at[first], m1.at[place1], up_sem.at[2, k], (partner, r))
    send(uw_hbm.at[first], w1.at[place1], up_sem.at[3, k], (partner, r))
    send(um_hbm.at[second], m2.at[here2], up_sem.at[0, place2], (partner, r))
    send(uw_hbm.at[second], w2.at[here2], up_sem.at[1, place2], (partner, r))

    def leaf_up(i, carry):
        for c in load(i):
            c.wait()
        solved = mul(dv[i], bv[i]).astype(BF)
        cl[i] = t_mul(solved, uv[i]).astype(BF)
        return carry

    lax.fori_loop(0, 4, leaf_up, 0)

    def node_up(pair, m, w):
        inner = mul_t(pair, m).astype(BF)
        return mul(inner, w).astype(BF)

    def local_up(i, carry):
        for c in load_local(i):
            c.wait()
        cn[i] = node_up(jnp.concatenate([cl[2 * i], cl[2 * i + 1]], axis=1), lm[i], lw[i])
        return carry

    lax.fori_loop(0, 2, local_up, 0)
    for c in load_local(2):
        c.wait()
    ct[...] = node_up(jnp.concatenate([cn[0], cn[1]], axis=1), lm[2], lw[2])

    send(ct.at[pl.ds(128 - 128 * k, 128)], p1.at[k], small_sem.at[0], (partner, r))
    p1[k] = ct[pl.ds(pl.multiple_of(128 * k, 128), 128), :]
    for c in own[:4]:
        c.wait()
    arrived(m1.at[pl.ds(256 - k * 256, 256)], up_sem.at[2, 1 - k])
    arrived(w1.at[pl.ds(256 - k * 256, 256)], up_sem.at[3, 1 - k])
    arrived(p1.at[1 - k], small_sem.at[0])
    c1[...] = node_up(jnp.concatenate([p1[0], p1[1]], axis=1), m1[...], w1[...])

    send(c1.at[pl.ds(64 - 64 * z0, 64)], p2.at[z0], small_sem.at[1], (across, r))
    p2[z0] = c1[pl.ds(pl.multiple_of(64 * z0, 64), 64), :]
    there2 = 2 - 2 * z0 + k
    there2_rows = pl.ds(there2 * 128, 128)
    arrived(m2.at[there2_rows], up_sem.at[0, there2])
    send(m2.at[there2_rows], m2.at[there2_rows], up_sem.at[0, there2], (partner, r))
    arrived(w2.at[there2_rows], up_sem.at[1, there2])
    send(w2.at[there2_rows], w2.at[there2_rows], up_sem.at[1, there2], (partner, r))
    relay(0, 1)
    relay(1, 1)
    ring_own(2)
    for c in (2 * z0 + 1 - k, 2 - 2 * z0 + 1 - k):
        rows = pl.ds(c * 128, 128)
        arrived(m2.at[rows], up_sem.at[0, c])
        arrived(w2.at[rows], up_sem.at[1, c])
    arrived(p2.at[1 - z0], small_sem.at[1])
    c2[...] = node_up(
        jnp.concatenate([p2[0], p2[1]], axis=1), m2[...], w2[...]
    ).reshape(4, 16, 256)

    for i in range(1, 4):
        h = lax.rem(g + i, 4)
        send(c2.at[h], p34.at[g], small_sem.at[2 + g], (4 * h + lax.rem(s, 4), r))
    p34[g] = c2[g]
    relay(0, 2)
    relay(1, 2)
    relay(2, 1)
    relay(0, 3)
    relay(1, 3)
    relay(0, 4)
    relay(1, 4)
    own[4].wait()
    own[5].wait()
    ring_rest(0)
    ring_rest(1)
    for i in range(1, 4):
        h = lax.rem(g + i, 4)
        arrived(p34.at[h], small_sem.at[2 + h])

    def m3(n):
        return rm[8 * n : 8 * n + 8, 0:64, :].reshape(512, 512)

    def w3(n):
        return rw[8 * n : 8 * n + 8, 0:64, :].reshape(512, 256)

    def m4():
        return rm[:, 64:96, :].reshape(512, 512)

    def w4():
        return rw[:, 64:96, :].reshape(512, 256)

    pairs = [jnp.concatenate([p34[2 * n], p34[2 * n + 1]], axis=1) for n in range(2)]
    c3 = [node_up(pairs[n], m3(n), w3(n)) for n in range(2)]
    inner4 = mul_t(jnp.concatenate(c3, axis=1), m4()).astype(BF)
    rt[r] = mul(inner4, w4()).astype(BF)

    for i in range(1, 16):
        send(rt.at[r], rt.at[r], root_sem.at[r], (s, lax.rem(r + i, 16)))

    for n in range(2):
        x = (pairs[n].astype(F32) - mul_t(inner4[:, 256 * n : 256 * n + 256], w3(n))).astype(BF)
        t2 = mul_t(x, m3(n)).astype(BF)
        t2s[2 * n] = t2[:, :256]
        t2s[2 * n + 1] = t2[:, 256:]
    for i in range(1, 4):
        h = lax.rem(g + i, 4)
        send(t2s.at[h], f2.at[g], small_sem.at[6 + g], (4 * h + lax.rem(s, 4), r))
    f2[g] = t2s[g]
    relay(2, 2)

    n_up = s // 8
    m4h = rm[pl.ds(8 * n_up, 8), 64:96, :].reshape(256, 512)
    e = mul(m4h, w4()).astype(BF)
    m3h = rm[pl.ds(4 * g, 4), 0:64, :].reshape(256, 512)
    w3h = rw[pl.ds(8 * n_up, 8), 0:64, :].reshape(512, 256)
    e = mul(m3h, mul(w3h, e).astype(BF)).astype(BF)
    m2h = m2[pl.ds(pl.multiple_of(256 * z0, 256), 256), :]
    e = mul(m2h, mul(w2[...], e).astype(BF)).astype(BF)
    m1h = m1[pl.ds(pl.multiple_of(256 * k, 256), 256), :]
    gq[...] = mul(m1h, mul(w1[...], e).astype(BF)).astype(BF)
    relay(2, 3)
    relay(2, 4)
    own[6].wait()
    ring_rest(2)

    for i in range(1, 16):
        q = lax.rem(r + i, 16)
        arrived(rt.at[q], root_sem.at[q])
    total = mul_t(rt[0], tp[0])
    for q in range(1, 16):
        total += mul_t(rt[q], tp[q])
    t4[slot] = total.astype(BF)
    for i in range(1, 16):
        send(t4.at[slot], t4.at[slot], t4_sem.at[slot], (lax.rem(s + i, 16), r))

    for i in range(1, 4):
        h = lax.rem(g + i, 4)
        arrived(f2.at[h], small_sem.at[6 + h])

    def node_down(pair, t, m, w):
        x = (pair.astype(F32) - mul_t(t, w)).astype(BF)
        return mul_t(x, m).astype(BF)

    t1 = node_down(
        jnp.concatenate([p2[0], p2[1]], axis=1), f2[...].reshape(64, 256), m2[...], w2[...]
    )
    t1s[0] = t1[:, :256]
    t1s[1] = t1[:, 256:]
    send(t1s.at[1 - z0], f1.at[z0], small_sem.at[10], (across, r))
    f1[z0] = t1s[z0]
    lo = mul(lm[2], mul(lw[2], gq[...]).astype(BF)).astype(BF)

    def down_gain(n, gain):
        e2 = mul(lm[n], mul(lw[n], gain).astype(BF)).astype(BF)
        for j in range(2):
            i = 2 * n + j
            ue = mul(uv[i], e2[256 * j : 256 * j + 256, :]).astype(BF)
            hv[i] = mul(dv[i], ue).astype(BF)

    down_gain(0, lo[:256])
    arrived(f1.at[1 - z0], small_sem.at[10])
    t0 = node_down(
        jnp.concatenate([p1[0], p1[1]], axis=1), f1[...].reshape(128, 256), m1[...], w1[...]
    )
    t0s[0] = t0[:, :256]
    t0s[1] = t0[:, 256:]
    send(t0s.at[1 - k], f0.at[k], small_sem.at[11], (partner, r))
    f0[k] = t0s[k]
    down_gain(1, lo[256:])
    arrived(f0.at[1 - k], small_sem.at[11])
    ta = node_down(
        jnp.concatenate([cn[0], cn[1]], axis=1), f0[...].reshape(256, 256), lm[2], lw[2]
    )
    for n in range(2):
        tb = node_down(
            jnp.concatenate([cl[2 * n], cl[2 * n + 1]], axis=1),
            ta[:, 256 * n : 256 * n + 256], lm[n], lw[n],
        )
        for j in range(2):
            i = 2 * n + j
            x = (bv[i].astype(F32) - mul_t(uv[i], tb[:, 256 * j : 256 * j + 256])).astype(BF)
            sv[i] = mul(dv[i], x)

    for i in range(1, 16):
        q = lax.rem(s + i, 16)
        q = 8 * lax.rem(q, 2) + 4 * lax.rem(q // 2, 2) + q // 4
        arrived(t4.at[q], t4_sem.at[q])
    top = t4[...].reshape(256, 256)

    def last(i):
        return pltpu.make_async_copy(sv.at[i], out_hbm.at[pl.ds(i * 512, 512)], out_sem.at[i])

    def finish(i, carry):
        sv[i] = sv[i] - mul_t(hv[i], top)
        last(i).start()
        return carry

    lax.fori_loop(0, 4, finish, 0)
    for copy in sent:
        copy.wait_send()
    for i in range(4):
        last(i).wait()


def body(b, d, u, lm, lw, um, uw, top):
    flat = [a.reshape(a.shape[-2:]) for a in (b, d, u, lm, lw, um, uw, top)]
    dma = pltpu.SemaphoreType.DMA
    vm = pltpu.VMEM
    out = pl.pallas_call(
        kernel,
        out_shape=jax.ShapeDtypeStruct((2048, 256), F32),
        in_specs=[pl.BlockSpec(memory_space=pl.ANY)] * 8,
        out_specs=pl.BlockSpec(memory_space=pl.ANY),
        scratch_shapes=[
            vm((4, 512, 256), BF), vm((4, 512, 512), BF), vm((4, 512, 256), BF),
            vm((3, 512, 512), BF), vm((3, 512, 256), BF),
            vm((512, 512), BF), vm((512, 256), BF), vm((512, 512), BF), vm((512, 256), BF),
            vm((16, 96, 512), BF), vm((16, 96, 256), BF), vm((16, 256, 256), BF),
            vm((4, 256, 256), BF), vm((2, 256, 256), BF), vm((256, 256), BF),
            vm((2, 128, 256), BF), vm((128, 256), BF), vm((2, 64, 256), BF), vm((4, 16, 256), BF),
            vm((4, 16, 256), BF), vm((16, 16, 256), BF), vm((16, 16, 256), BF),
            vm((4, 16, 256), BF), vm((4, 16, 256), BF), vm((2, 64, 256), BF), vm((2, 64, 256), BF),
            vm((2, 128, 256), BF), vm((2, 128, 256), BF), vm((256, 256), BF),
            vm((4, 512, 256), F32), vm((4, 512, 256), BF),
            dma((5, 4)), dma((7,)), dma((4,)), dma((104,)), dma((4, 4)), dma((3, 16)),
            dma((12,)), dma((16,)), dma((16,)),
        ],
        compiler_params=pltpu.CompilerParams(
            collective_id=0, has_side_effects=True, vmem_limit_bytes=56 << 20
        ),
    )(*flat)
    return out.reshape(1, 2048, 256)


def solution(mesh):
    rows = P("root", "sub", None)
    return jax.shard_map(
        body, mesh=mesh, in_specs=(rows,) * 7 + (P("root", "sub"),), out_specs=rows, check_vma=False
    )
```

time: 242 us -> 67.8 us (0.28)
  waiting for transfers between devices: 139 us -> 0 us
  Pallas kernels: 0 us -> 64.6 us
  matrix products: 40 us -> 0 us
  local copies, waits for them, and re-layouts: 34.7 us -> 3.05 us
  between operations: 13.5 us -> 0.01 us
  starting transfers between devices: 6.68 us -> 0 us
  blocking collectives: 4.96 us -> 0 us
    all_gather x3 -> x0, waiting for transfers between devices: 107 us -> none  [the longest x1 68.7 us: side_by_side(): filled = lax.all_gather(both, axis, axis=dim, tiled=True)]
    pallas_call x0 -> x1, Pallas kernels: none -> 64.6 us  [body(): pl.pallas_call(kernel, out_shape=jax.ShapeDtypeStruct((2048, 256), F32),...]
    dot_general x22 -> x0, matrix products: 40 us -> none  [the longest x14 32.2 us: batch_product(): jnp.einsum('nij,njk->nik', left, right, preferred_element_type=jnp.float32)]
    all_to_all x1 -> x0, waiting for transfers between devices: 32.6 us -> none  [from_everyone(): lax.all_to_all(jnp.broadcast_to(shard[None], (length, *shard.shape)), axi...]
    slice x10 -> x0, local copies, waits for them, and re-layouts: 12 us -> none  [the longest x4 8.2 us: body(): all_rows[:, offset:offset + height]]
    split x2 -> x0, local copies, waits for them, and re-layouts: 10.2 us -> none  [side_by_side(): jnp.split(filled, [sum(widths[:k]) for k in range(1, len(widths))], axis=...]
    all_to_all x1 -> x0, starting transfers between devices: 6.6 us -> none  [from_everyone(): lax.all_to_all(jnp.broadcast_to(shard[None], (length, *shard.shape)), axi...]
    all_gather x1 -> x0, blocking collectives: 4.96 us -> none  [whole_of(): nearer = lax.all_gather(shard, axes[-1], axis=dim, tiled=True)]
  transfers between devices with their start and end apart: 4 -> 0, of which waited for: 4 -> 0; matrix products, arithmetic and copies ran while one was open for 13% -> 0% of each run, Pallas kernels for 0% -> 0%
where the time goes in v1:
time: 67.8 us; the launch traced here: 67.7 us
  Pallas kernels  64.6 us (95%)
  local copies, waits for them, and re-layouts  3.05 us (4%)
    pallas_call x1, Pallas kernels, body(): pl.pallas_call(kernel, out_shape=jax.ShapeDtypeStruct((2048, 256), F32),...  64.6 us
    unnamed x1, local copies, waits for them, and re-layouts  3.05 us

profile of v1, /device:TPU:1, one launch (start us, length us, event | category | flops | bytes accessed | tf_op | source)
XLA Modules:
  0.0 67.7 jit_solution(18103725304813224971)
XLA Ops:
  0.0 64.6 %shard_map.82 = f32[2048,256]{1,0:T(8,128)} custom-call(bf16[2048,256]{1,0:T(8,128)(2,1)} %bitcast.11, bf16[2048,512]{1,0:T(8,128)(2,1)} %bitcast.9, bf16[2048,256]{1,0:T(8,128)(2,1)} %bitcast.12, bf16[1536,512]{1,0:T(8,128)(2,1)} %bitcast.10, bf16[1536,256]{1,0:T(8,128)(2,1)} %bitcast.13, bf16[480,512]{1,0:T(8,128)(2,1)} %bitcast.14, ...), custom_call_target="tpu_custom_call" | custom-call | tf_op jit(solution)/shard_map/pallas_call | solution.py:346
  64.6 3.0 %copy.10 = f32[1,2048,256]{2,1,0:T(8,128)} copy(f32[1,2048,256]{2,1,0:T(8,128)} %bitcast.8) | data formatting | bytes 4194304

commit v2 on v1

v2 whole, which is shorter than its diff:
```python
import jax
import jax.numpy as jnp
from jax import lax
from jax.experimental import pallas as pl
from jax.experimental.pallas import tpu as pltpu
from jax.sharding import PartitionSpec as P

MESH = pl.DeviceIdType.MESH
BF = jnp.bfloat16
F32 = jnp.float32


def mul(a, b):
    return lax.dot_general(a, b, (((1,), (0,)), ((), ())), preferred_element_type=F32)


def mul_t(a, b):
    return lax.dot_general(a, b, (((1,), (1,)), ((), ())), preferred_element_type=F32)


def t_mul(a, b):
    return lax.dot_general(a, b, (((0,), (0,)), ((), ())), preferred_element_type=F32)


class V:
    def __init__(self, ref, index=None):
        self.ref, self.index = ref, index

    def __getitem__(self, index):
        return V(self.ref, index)


def at(view):
    return view.ref.at[view.index] if isinstance(view, V) else view


def kernel(
    b_hbm, d_hbm, u_hbm, lm_hbm, lw_hbm, um_hbm, uw_hbm, top_hbm,
    out_hbm,
    bv, dv, uv, lm, lw, m1, w1, m2, w2, rm, rw, xm, xw, tp,
    cl, cn, ct, p1, p2, c1, c2, p3, p4, rt, t4,
    t2s, f2, t1s, f1, t0s, f0, ks, kr, sv, hv,
    load_sem, own_sem, out_sem, both_sem, proc_sem, edge_sem, root_send_sem,
    up_sem, ring_sem, small_sem, root_sem, t4_sem,
):
    s = lax.axis_index("sub")
    r = lax.axis_index("root")
    k = lax.rem(s, 2)
    q = lax.rem(s // 2, 4)
    is_proc = lax.rem((q + 1) // 2, 2)
    side_no = q // 2
    child = 1 - side_no
    n = s // 8
    slot = 4 * n + 2 * k + side_no
    partner = s + 1 - 2 * k
    near_slots = [4 * n + 2 * k + child, 4 - 4 * n + 2 * k + side_no, 4 - 4 * n + 2 * k + child]
    edge = s + 4 * side_no - 2
    mate = s + 2 - 4 * side_no
    mate_edge = s + 4 - 8 * side_no
    opposite = lax.rem(s + 8, 16)
    cross = 14 - s + 2 * k
    base = 8 * n
    ids = {
        "own": (s, s - base), "edge": (edge, edge - base),
        "mate": (mate, mate - base), "mate_edge": (mate_edge, mate_edge - base),
        "x_own": (cross, 0), "x_edge": (cross + 2 - 4 * side_no, 0),
        "x_mate": (cross - 2 + 4 * side_no, 0), "x_mate_edge": (cross - 4 + 8 * side_no, 0),
    }
    column = [lax.rem(s + i, 16) for i in range(16)]
    plane = [lax.rem(r + i, 16) for i in range(16)]
    eighth = [lax.rem(r + i, 8) for i in range(8)]
    root_home = r // 8 == n

    barrier = pltpu.get_barrier_semaphore()
    for i in range(1, 16):
        pl.semaphore_signal(barrier, inc=1, device_id=(column[i], r), device_id_type=MESH)
    for i in range(1, 16):
        pl.semaphore_signal(barrier, inc=1, device_id=(s, plane[i]), device_id_type=MESH)

    def load(i):
        rows = pl.ds(i * 512, 512)
        return [
            pltpu.make_async_copy(d_hbm.at[rows], dv.at[i], load_sem.at[0, i]),
            pltpu.make_async_copy(b_hbm.at[rows], bv.at[i], load_sem.at[1, i]),
            pltpu.make_async_copy(u_hbm.at[rows], uv.at[i], load_sem.at[2, i]),
        ]

    def load_local(i):
        rows = pl.ds(i * 512, 512)
        return [
            pltpu.make_async_copy(lm_hbm.at[rows], lm.at[i], load_sem.at[3, i]),
            pltpu.make_async_copy(lw_hbm.at[rows], lw.at[i], load_sem.at[4, i]),
        ]

    for i in range(4):
        for c in load(i):
            c.start()
    for i in range(3):
        for c in load_local(i):
            c.start()
    place1 = pl.ds(k * 256, 256)
    other1 = pl.ds(256 - k * 256, 256)
    own2 = 2 * child + k
    beside2 = 2 * child + 1 - k
    edge2 = 2 - 2 * child + k
    beside_edge2 = 3 - 2 * child - k
    from_edge2 = 2 * side_no + k

    def part2(i):
        return pl.ds(i * 128, 128)

    here2 = part2(own2)
    edge_rows2 = part2(edge2)
    to_proc2 = part2(from_edge2)
    mate_set = pl.ds(64 - 64 * side_no, 64)
    first, second, third, fourth = pl.ds(0, 256), pl.ds(256, 128), pl.ds(384, 64), pl.ds(448, 32)
    own = [
        pltpu.make_async_copy(um_hbm.at[first], m1.at[place1], own_sem.at[0]),
        pltpu.make_async_copy(uw_hbm.at[first], w1.at[place1], own_sem.at[1]),
        pltpu.make_async_copy(um_hbm.at[second], m2.at[here2], own_sem.at[2]),
        pltpu.make_async_copy(uw_hbm.at[second], w2.at[here2], own_sem.at[3]),
        pltpu.make_async_copy(um_hbm.at[third], rm.at[s - base], own_sem.at[4]),
        pltpu.make_async_copy(uw_hbm.at[third], rw.at[s - base], own_sem.at[5]),
        pltpu.make_async_copy(um_hbm.at[fourth], xm.at[s], own_sem.at[6]),
        pltpu.make_async_copy(uw_hbm.at[fourth], xw.at[s], own_sem.at[7]),
        pltpu.make_async_copy(top_hbm, tp.at[s - base], own_sem.at[8]),
    ]
    for c in own:
        c.start()

    sent = {0: [], 1: [], 2: [], 3: []}
    sems = {0: proc_sem, 1: edge_sem, 2: both_sem, 3: root_send_sem}

    def copy_of(which, i):
        src, dst, sem, to = sent[which][i]
        src, dst, sem = at(src), at(dst), at(sem)
        return pltpu.make_async_remote_copy(
            src_ref=src, dst_ref=dst, send_sem=sems[which].at[i], recv_sem=sem,
            device_id=to, device_id_type=MESH,
        )

    def send(which, src, dst, sem, to):
        sent[which].append((src, dst, sem, to))
        copy_of(which, len(sent[which]) - 1).start()
        return len(sent[which]) - 1

    flushed = set()

    def flush(which, copies):
        for i in copies:
            copy_of(which, i).wait_send()
            flushed.add((which, i))

    def drain(which):
        for i in range(len(sent[which])):
            if (which, i) not in flushed:
                copy_of(which, i).wait_send()

    def arrived(dst, sem):
        pltpu.make_async_remote_copy(
            src_ref=dst, dst_ref=dst, send_sem=both_sem.at[0], recv_sem=sem,
            device_id=(partner, r), device_id_type=MESH,
        ).wait_recv()

    pl.semaphore_wait(barrier, 30)

    rings = (
        (V(um_hbm)[third], rm, 1), (V(uw_hbm)[third], rw, 1),
        (V(um_hbm)[fourth], xm, 0), (V(uw_hbm)[fourth], xw, 0), (top_hbm, tp, 1),
    )

    def spot(a, name):
        i = ids[name][rings[a][2]]
        return V(rings[a][1])[i], V(ring_sem)[a, i]

    def ring_own(which, arrays, to):
        for a in arrays:
            dst, sem = spot(a, "own")
            send(which, rings[a][0], dst, sem, (to, r))

    def relay(name, arrays, *to):
        for a in arrays:
            dst, sem = spot(a, name)
            arrived(at(dst), at(sem))
            for t in to:
                send(0, dst, dst, sem, (t, r))

    @pl.when(is_proc == 0)
    def _():
        send(1, V(um_hbm)[second], V(m2)[to_proc2], V(up_sem)[0, 2], (mate, r))
        send(1, V(uw_hbm)[second], V(w2)[to_proc2], V(up_sem)[1, 2], (mate, r))
        ring_own(1, (0, 1), mate)

    @pl.when(is_proc == 1)
    def _():
        ring_own(0, (0, 1, 2, 3), mate)
        ring_own(0, (2, 3), cross)

    send(2, V(um_hbm)[first], V(m1)[place1], V(up_sem)[2, 0], (partner, r))
    send(2, V(uw_hbm)[first], V(w1)[place1], V(up_sem)[3, 0], (partner, r))

    @pl.when(is_proc == 1)
    def _():
        send(0, V(um_hbm)[second], V(m2)[here2], V(up_sem)[0, 1], (partner, r))
        send(0, V(uw_hbm)[second], V(w2)[here2], V(up_sem)[1, 1], (partner, r))
        ring_own(0, (0, 1, 2, 3, 4), partner)
        ring_own(0, (4,), mate)

    def leaf_up(i, carry):
        for c in load(i):
            c.wait()
        solved = mul(dv[i], bv[i]).astype(BF)
        cl[i] = t_mul(solved, uv[i]).astype(BF)
        return carry

    lax.fori_loop(0, 4, leaf_up, 0)

    def node_up(pair, m, w):
        inner = mul_t(pair, m).astype(BF)
        return mul(inner, w).astype(BF)

    def node_down(pair, t, m, w):
        x = (pair.astype(F32) - mul_t(t, w)).astype(BF)
        return mul_t(x, m).astype(BF)

    def side(ref, i):
        return jnp.concatenate([ref[2 * i], ref[2 * i + 1]], axis=1)

    def local_up(i, carry):
        for c in load_local(i):
            c.wait()
        cn[i] = node_up(side(cl, i), lm[i], lw[i])
        return carry

    lax.fori_loop(0, 2, local_up, 0)
    for c in load_local(2):
        c.wait()
    ct[...] = node_up(side(cn, 0), lm[2], lw[2])

    send(2, V(ct)[pl.ds(128 - 128 * k, 128)], V(p1)[k], V(small_sem)[0], (partner, r))
    p1[k] = ct[pl.ds(pl.multiple_of(128 * k, 128), 128), :]
    for c in own:
        c.wait()
    arrived(m1.at[other1], up_sem.at[2, 0])
    arrived(w1.at[other1], up_sem.at[3, 0])
    arrived(p1.at[1 - k], small_sem.at[0])
    c1[...] = node_up(side(p1, 0), m1[...], w1[...])

    def own_gain(e):
        m1h = m1[pl.ds(pl.multiple_of(256 * k, 256), 256), :]
        e = mul(m1h, mul(w1[...], e).astype(BF)).astype(BF)
        lo = mul(lm[2], mul(lw[2], e).astype(BF)).astype(BF)
        for n in range(2):
            half = lo[256 * n : 256 * n + 256]
            e2 = mul(lm[n], mul(lw[n], half).astype(BF)).astype(BF)
            for j in range(2):
                i = 2 * n + j
                ue = mul(uv[i], e2[256 * j : 256 * j + 256, :]).astype(BF)
                hv[i] = mul(dv[i], ue).astype(BF)

    @pl.when(is_proc == 0)
    def _():
        send(1, c1, V(p2)[side_no], V(small_sem)[1], (mate, r))
        ring_own(1, (2, 3, 4), mate)
        arrived(kr, small_sem.at[10])
        own_gain(kr[...])
        arrived(f1, small_sem.at[11])

    @pl.when(is_proc == 1)
    def _():
        p2[child] = c1[...]
        arrived(m2.at[part2(edge2)], up_sem.at[0, 2])
        send(0, V(m2)[edge_rows2], V(m2)[edge_rows2], V(up_sem)[0, 3], (partner, r))
        arrived(w2.at[part2(edge2)], up_sem.at[1, 2])
        send(0, V(w2)[edge_rows2], V(w2)[edge_rows2], V(up_sem)[1, 3], (partner, r))
        relay("mate", (0, 1), partner)
        relay("mate", (2, 3), partner, cross)
        relay("edge", (0, 1), mate, partner)
        for i, c in ((1, beside2), (3, beside_edge2)):
            arrived(m2.at[part2(c)], up_sem.at[0, i])
            arrived(w2.at[part2(c)], up_sem.at[1, i])
        arrived(p2.at[1 - child], small_sem.at[1])
        c2[...] = node_up(side(p2, 0), m2[...], w2[...])
        send(0, V(c2)[mate_set], V(p3)[side_no], V(small_sem)[2], (mate, r))
        p3[side_no] = c2[pl.ds(pl.multiple_of(64 * side_no, 64), 64), :]
        relay("edge", (2, 3), mate, partner, cross)
        relay("mate_edge", (0, 1), partner)
        for a in (0, 1):
            for i in range(4):
                j = lax.rem(partner + 2 * i, 8)
                arrived(rings[a][1].at[j], ring_sem.at[a, j])
        arrived(p3.at[1 - side_no], small_sem.at[2])
        m3 = rm[...].reshape(512, 512)
        w3 = rw[...].reshape(512, 256)
        pair3 = side(p3, 0)
        p4[n] = node_up(pair3, m3, w3)
        send(0, V(p4)[n], V(p4)[n], V(small_sem)[3], (opposite, r))
        relay("mate_edge", (2, 3), partner, cross)
        relay("edge", (4,), mate, partner)
        relay("mate", (4,), partner)
        for name in ("x_own", "x_mate", "x_edge", "x_mate_edge"):
            relay(name, (2, 3), partner)
        for a in (2, 3):
            for i in range(8):
                j = lax.rem(partner + 2 * i, 16)
                arrived(rings[a][1].at[j], ring_sem.at[a, j])
        arrived(p4.at[1 - n], small_sem.at[3])
        w4 = xw[...].reshape(512, 256)
        inner4 = mul_t(side(p4, 0), xm[...].reshape(512, 512)).astype(BF)
        root = mul(inner4, w4).astype(BF)

        @pl.when(root_home)
        def _():
            rt[eighth[0]] = root
            for i in range(1, 16):
                send(3, V(rt)[eighth[0]], V(rt)[eighth[0]], V(root_sem)[eighth[0]], (s, plane[i]))

        t3 = jnp.where(n == 0, inner4[:, :256], inner4[:, 256:])
        t2 = node_down(pair3, t3, m3, w3)
        t2s[0] = t2[:, :256]
        t2s[1] = t2[:, 256:]
        send(0, V(t2s)[child], V(f2)[side_no], V(small_sem)[6], (mate, r))
        f2[side_no] = t2s[side_no]
        relay("mate_edge", (4,), partner)

        m4h = xm[pl.ds(base, 8)].reshape(256, 512)
        e = mul(m4h, w4).astype(BF)
        m3h = rm[pl.ds(4 * side_no, 4)].reshape(256, 512)
        e = mul(m3h, mul(w3, e).astype(BF)).astype(BF)
        lifted2 = mul(w2[...], e).astype(BF)
        m2_edge = m2[pl.ds(pl.multiple_of(256 - 256 * child, 256), 256), :]
        ks[...] = mul(m2_edge, lifted2).astype(BF)
        send(0, ks, kr, V(small_sem)[10], (edge, r))
        m2_own = m2[pl.ds(pl.multiple_of(256 * child, 256), 256), :]
        own_gain(mul(m2_own, lifted2).astype(BF))
        arrived(f2.at[child], small_sem.at[6])
        t1 = node_down(side(p2, 0), f2[...].reshape(128, 256), m2[...], w2[...])
        t1s[0] = t1[:, :256]
        t1s[1] = t1[:, 256:]
        send(0, V(t1s)[side_no], f1, V(small_sem)[11], (edge, r))
        f1[...] = t1s[child]
        for i in range(4):
            j = lax.rem(partner + 2 * i, 8)
            arrived(tp.at[j], ring_sem.at[4, j])

        for i in range(1, 8):
            arrived(rt.at[eighth[i]], root_sem.at[eighth[i]])

        @pl.when(jnp.logical_not(root_home))
        def _():
            arrived(rt.at[eighth[0]], root_sem.at[eighth[0]])

        total = mul_t(rt[0], tp[0])
        for j in range(1, 8):
            total += mul_t(rt[j], tp[j])
        t4[slot] = total.astype(BF)
        for i in range(1, 8):
            send(0, V(t4)[slot], V(t4)[slot], V(t4_sem)[slot], (column[2 * i], r))
        send(0, V(t4)[slot], V(t4)[slot], V(t4_sem)[slot], (partner, r))

    t0 = node_down(side(p1, 0), f1[...], m1[...], w1[...])
    t0s[0] = t0[:, :256]
    t0s[1] = t0[:, 256:]
    send(2, V(t0s)[1 - k], V(f0)[k], V(small_sem)[12], (partner, r))
    f0[k] = t0s[k]
    arrived(f0.at[1 - k], small_sem.at[12])
    ta = node_down(side(cn, 0), f0[...].reshape(256, 256), lm[2], lw[2])
    for n in range(2):
        tb = node_down(side(cl, n), ta[:, 256 * n : 256 * n + 256], lm[n], lw[n])
        for j in range(2):
            i = 2 * n + j
            x = (bv[i].astype(F32) - mul_t(uv[i], tb[:, 256 * j : 256 * j + 256])).astype(BF)
            sv[i] = mul(dv[i], x)

    def pass_on(which, i):
        arrived(t4.at[i], t4_sem.at[i])
        send(which, V(t4)[i], V(t4)[i], V(t4_sem)[i], (partner, r))

    @pl.when(is_proc == 0)
    def _():
        pass_on(1, slot)

    for i in near_slots:
        pass_on(2, i)
    for i in range(4):
        j = 4 * (i // 2) + 2 - 2 * k + i % 2
        arrived(t4.at[j], t4_sem.at[j])

    top = (t4[0:4].astype(F32) + t4[4:8].astype(F32)).astype(BF).reshape(256, 256)

    def last(i):
        return pltpu.make_async_copy(sv.at[i], out_hbm.at[pl.ds(i * 512, 512)], out_sem.at[i])

    def finish(i, carry):
        sv[i] = sv[i] - mul_t(hv[i], top)
        last(i).start()
        return carry

    lax.fori_loop(0, 4, finish, 0)
    drain(2)

    @pl.when(is_proc == 1)
    def _():
        drain(0)

        @pl.when(root_home)
        def _():
            drain(3)

    @pl.when(is_proc == 0)
    def _():
        drain(1)

    for i in range(4):
        last(i).wait()


def body(b, d, u, lm, lw, um, uw, top):
    flat = [a.reshape(a.shape[-2:]) for a in (b, d, u, lm, lw, um, uw, top)]
    dma = pltpu.SemaphoreType.DMA
    vm = pltpu.VMEM
    out = pl.pallas_call(
        kernel,
        out_shape=jax.ShapeDtypeStruct((2048, 256), F32),
        in_specs=[pl.BlockSpec(memory_space=pl.ANY)] * 8,
        out_specs=pl.BlockSpec(memory_space=pl.ANY),
        scratch_shapes=[
            vm((4, 512, 256), BF), vm((4, 512, 512), BF), vm((4, 512, 256), BF),
            vm((3, 512, 512), BF), vm((3, 512, 256), BF),
            vm((512, 512), BF), vm((512, 256), BF), vm((512, 512), BF), vm((512, 256), BF),
            vm((8, 64, 512), BF), vm((8, 64, 256), BF), vm((16, 32, 512), BF), vm((16, 32, 256), BF),
            vm((8, 256, 256), BF),
            vm((4, 256, 256), BF), vm((2, 256, 256), BF), vm((256, 256), BF),
            vm((2, 128, 256), BF), vm((2, 128, 256), BF), vm((128, 256), BF), vm((128, 256), BF),
            vm((2, 64, 256), BF), vm((2, 64, 256), BF), vm((8, 64, 256), BF), vm((8, 64, 256), BF),
            vm((2, 64, 256), BF), vm((2, 64, 256), BF), vm((2, 128, 256), BF), vm((128, 256), BF),
            vm((2, 128, 256), BF), vm((2, 128, 256), BF), vm((256, 256), BF), vm((256, 256), BF),
            vm((4, 512, 256), F32), vm((4, 512, 256), BF),
            dma((5, 4)), dma((9,)), dma((4,)), dma((7,)), dma((92,)), dma((9,)), dma((15,)),
            dma((4, 4)), dma((5, 16)), dma((13,)), dma((8,)), dma((8,)),
        ],
        compiler_params=pltpu.CompilerParams(
            collective_id=0, has_side_effects=True, vmem_limit_bytes=56 << 20
        ),
    )(*flat)
    return out.reshape(1, 2048, 256)


def solution(mesh):
    rows = P("root", "sub", None)
    return jax.shard_map(
        body, mesh=mesh, in_specs=(rows,) * 7 + (P("root", "sub"),), out_specs=rows, check_vma=False
    )
```

time: 67.8 us -> 56.6 us (0.83)
  Pallas kernels: 64.6 us -> 53.5 us
    pallas_call x1, Pallas kernels: 64.6 us -> 53.5 us  [body(): pl.pallas_call(kernel, out_shape=jax.ShapeDtypeStruct((2048, 256), F32),...]
where the time goes in v2:
time: 56.6 us; the launch traced here: 56.5 us
  Pallas kernels  53.5 us (95%)
  local copies, waits for them, and re-layouts  3.05 us (5%)
    pallas_call x1, Pallas kernels, body(): pl.pallas_call(kernel, out_shape=jax.ShapeDtypeStruct((2048, 256), F32),...  53.5 us
    unnamed x1, local copies, waits for them, and re-layouts  3.05 us

profile of v2, /device:TPU:1, one launch (start us, length us, event | category | flops | bytes accessed | tf_op | source)
XLA Modules:
  0.0 56.5 jit_solution(5612318682431439759)
XLA Ops:
  0.0 53.5 %shard_map.82 = f32[2048,256]{1,0:T(8,128)} custom-call(bf16[2048,256]{1,0:T(8,128)(2,1)} %bitcast.11, bf16[2048,512]{1,0:T(8,128)(2,1)} %bitcast.9, bf16[2048,256]{1,0:T(8,128)(2,1)} %bitcast.12, bf16[1536,512]{1,0:T(8,128)(2,1)} %bitcast.10, bf16[1536,256]{1,0:T(8,128)(2,1)} %bitcast.13, bf16[480,512]{1,0:T(8,128)(2,1)} %bitcast.14, ...), custom_call_target="tpu_custom_call" | custom-call | tf_op jit(solution)/shard_map/pallas_call | solution.py:422
  53.5 3.0 %copy.10 = f32[1,2048,256]{2,1,0:T(8,128)} copy(f32[1,2048,256]{2,1,0:T(8,128)} %bitcast.8) | data formatting | bytes 4194304

commit v3 on v2

--- a/solution.py
+++ b/solution.py
@@ -36,11 +36,11 @@
 
 def kernel(
     b_hbm, d_hbm, u_hbm, lm_hbm, lw_hbm, um_hbm, uw_hbm, top_hbm,
-    out_hbm,
+    sv, hv, top,
     bv, dv, uv, lm, lw, m1, w1, m2, w2, rm, rw, xm, xw, tp,
     cl, cn, ct, p1, p2, c1, c2, p3, p4, rt, t4,
-    t2s, f2, t1s, f1, t0s, f0, ks, kr, sv, hv,
-    load_sem, own_sem, out_sem, both_sem, proc_sem, edge_sem, root_send_sem,
+    t2s, f2, t1s, f1, t0s, f0, ks, kr,
+    load_sem, own_sem, both_sem, proc_sem, edge_sem, root_send_sem,
     up_sem, ring_sem, small_sem, root_sem, t4_sem,
 ):
     s = lax.axis_index("sub")
@@ -60,6 +60,7 @@
     opposite = lax.rem(s + 8, 16)
     cross = 14 - s + 2 * k
     base = 8 * n
+    far = lax.rem(s + 12 + 8 * side_no, 16)
     ids = {
         "own": (s, s - base), "edge": (edge, edge - base),
         "mate": (mate, mate - base), "mate_edge": (mate_edge, mate_edge - base),
@@ -67,14 +68,18 @@
         "x_mate": (cross - 2 + 4 * side_no, 0), "x_mate_edge": (cross - 4 + 8 * side_no, 0),
     }
     column = [lax.rem(s + i, 16) for i in range(16)]
-    plane = [lax.rem(r + i, 16) for i in range(16)]
+    far_first = sorted(
+        [(dy, dx) for dy in range(4) for dx in range(4) if dy or dx],
+        key=lambda d: -min(d[0], 4 - d[0]) - min(d[1], 4 - d[1]),
+    )
+    plane = [4 * lax.rem(r // 4 + dy, 4) + lax.rem(r + dx, 4) for dy, dx in far_first]
     eighth = [lax.rem(r + i, 8) for i in range(8)]
     root_home = r // 8 == n
 
     barrier = pltpu.get_barrier_semaphore()
     for i in range(1, 16):
         pl.semaphore_signal(barrier, inc=1, device_id=(column[i], r), device_id_type=MESH)
-    for i in range(1, 16):
+    for i in range(15):
         pl.semaphore_signal(barrier, inc=1, device_id=(s, plane[i]), device_id_type=MESH)
 
     def load(i):
@@ -187,9 +192,10 @@
 
     @pl.when(is_proc == 0)
     def _():
+        ring_own(1, (0, 1), mate)
         send(1, V(um_hbm)[second], V(m2)[to_proc2], V(up_sem)[0, 2], (mate, r))
         send(1, V(uw_hbm)[second], V(w2)[to_proc2], V(up_sem)[1, 2], (mate, r))
-        ring_own(1, (0, 1), mate)
+        ring_own(1, (2, 3), far)
 
     @pl.when(is_proc == 1)
     def _():
@@ -260,7 +266,8 @@
 
     @pl.when(is_proc == 0)
     def _():
-        send(1, c1, V(p2)[side_no], V(small_sem)[1], (mate, r))
+        first_sent = send(1, c1, V(p2)[side_no], V(small_sem)[1], (mate, r))
+        flush(1, [first_sent])
         ring_own(1, (2, 3, 4), mate)
         arrived(kr, small_sem.at[10])
         own_gain(kr[...])
@@ -269,13 +276,15 @@
     @pl.when(is_proc == 1)
     def _():
         p2[child] = c1[...]
+        relay("edge", (0, 1), mate, partner)
         arrived(m2.at[part2(edge2)], up_sem.at[0, 2])
         send(0, V(m2)[edge_rows2], V(m2)[edge_rows2], V(up_sem)[0, 3], (partner, r))
         arrived(w2.at[part2(edge2)], up_sem.at[1, 2])
         send(0, V(w2)[edge_rows2], V(w2)[edge_rows2], V(up_sem)[1, 3], (partner, r))
         relay("mate", (0, 1), partner)
-        relay("mate", (2, 3), partner, cross)
-        relay("edge", (0, 1), mate, partner)
+        relay("mate", (2, 3), partner)
+        relay("x_own", (2, 3), mate, partner)
+        relay("x_edge", (2, 3), mate, partner)
         for i, c in ((1, beside2), (3, beside_edge2)):
             arrived(m2.at[part2(c)], up_sem.at[0, i])
             arrived(w2.at[part2(c)], up_sem.at[1, i])
@@ -283,7 +292,6 @@
         c2[...] = node_up(side(p2, 0), m2[...], w2[...])
         send(0, V(c2)[mate_set], V(p3)[side_no], V(small_sem)[2], (mate, r))
         p3[side_no] = c2[pl.ds(pl.multiple_of(64 * side_no, 64), 64), :]
-        relay("edge", (2, 3), mate, partner, cross)
         relay("mate_edge", (0, 1), partner)
         for a in (0, 1):
             for i in range(4):
@@ -295,11 +303,11 @@
         pair3 = side(p3, 0)
         p4[n] = node_up(pair3, m3, w3)
         send(0, V(p4)[n], V(p4)[n], V(small_sem)[3], (opposite, r))
-        relay("mate_edge", (2, 3), partner, cross)
+        relay("x_mate", (2, 3), partner)
+        relay("x_mate_edge", (2, 3), partner)
+        relay("edge", (2, 3), mate, partner)
         relay("edge", (4,), mate, partner)
-        relay("mate", (4,), partner)
-        for name in ("x_own", "x_mate", "x_edge", "x_mate_edge"):
-            relay(name, (2, 3), partner)
+        relay("mate_edge", (2, 3), partner)
         for a in (2, 3):
             for i in range(8):
                 j = lax.rem(partner + 2 * i, 16)
@@ -312,7 +320,7 @@
         @pl.when(root_home)
         def _():
             rt[eighth[0]] = root
-            for i in range(1, 16):
+            for i in range(15):
                 send(3, V(rt)[eighth[0]], V(rt)[eighth[0]], V(root_sem)[eighth[0]], (s, plane[i]))
 
         t3 = jnp.where(n == 0, inner4[:, :256], inner4[:, 256:])
@@ -321,6 +329,7 @@
         t2s[1] = t2[:, 256:]
         send(0, V(t2s)[child], V(f2)[side_no], V(small_sem)[6], (mate, r))
         f2[side_no] = t2s[side_no]
+        relay("mate", (4,), partner)
         relay("mate_edge", (4,), partner)
 
         m4h = xm[pl.ds(base, 8)].reshape(256, 512)
@@ -354,7 +363,7 @@
         for j in range(1, 8):
             total += mul_t(rt[j], tp[j])
         t4[slot] = total.astype(BF)
-        for i in range(1, 8):
+        for i in (4, 3, 5, 2, 6, 1, 7):
             send(0, V(t4)[slot], V(t4)[slot], V(t4_sem)[slot], (column[2 * i], r))
         send(0, V(t4)[slot], V(t4)[slot], V(t4_sem)[slot], (partner, r))
 
@@ -386,17 +395,7 @@
         j = 4 * (i // 2) + 2 - 2 * k + i % 2
         arrived(t4.at[j], t4_sem.at[j])
 
-    top = (t4[0:4].astype(F32) + t4[4:8].astype(F32)).astype(BF).reshape(256, 256)
-
-    def last(i):
-        return pltpu.make_async_copy(sv.at[i], out_hbm.at[pl.ds(i * 512, 512)], out_sem.at[i])
-
-    def finish(i, carry):
-        sv[i] = sv[i] - mul_t(hv[i], top)
-        last(i).start()
-        return carry
-
-    lax.fori_loop(0, 4, finish, 0)
+    top[...] = (t4[0:4].astype(F32) + t4[4:8].astype(F32)).astype(BF).reshape(256, 256)
     drain(2)
 
     @pl.when(is_proc == 1)
@@ -411,19 +410,38 @@
     def _():
         drain(1)
 
-    for i in range(4):
+
+def final_kernel(sv, hv, top, out_hbm, ov, out_sem):
+    def last(i):
+        return pltpu.make_async_copy(ov.at[i], out_hbm.at[pl.ds(i * 256, 256)], out_sem.at[i])
+
+    def finish(i, carry):
+        rows = pl.ds(pl.multiple_of(256 * lax.rem(i, 2), 256), 256)
+        ov[i] = sv[i // 2, rows, :] - mul_t(hv[i // 2, rows, :], top[...])
+        last(i).start()
+        return carry
+
+    lax.fori_loop(0, 8, finish, 0)
+    for i in range(8):
         last(i).wait()
 
 
 def body(b, d, u, lm, lw, um, uw, top):
-    flat = [a.reshape(a.shape[-2:]) for a in (b, d, u, lm, lw, um, uw, top)]
+    flat = [
+        pltpu.with_memory_space_constraint(a.reshape(a.shape[-2:]), pltpu.HBM)
+        for a in (b, d, u, lm, lw, um, uw, top)
+    ]
     dma = pltpu.SemaphoreType.DMA
     vm = pltpu.VMEM
-    out = pl.pallas_call(
+    inside = pl.BlockSpec(memory_space=pltpu.VMEM)
+    parts = pl.pallas_call(
         kernel,
-        out_shape=jax.ShapeDtypeStruct((2048, 256), F32),
-        in_specs=[pl.BlockSpec(memory_space=pl.ANY)] * 8,
-        out_specs=pl.BlockSpec(memory_space=pl.ANY),
+        out_shape=(
+            jax.ShapeDtypeStruct((4, 512, 256), F32), jax.ShapeDtypeStruct((4, 512, 256), BF),
+            jax.ShapeDtypeStruct((256, 256), BF),
+        ),
+        in_specs=[pl.BlockSpec(memory_space=pltpu.HBM)] * 8,
+        out_specs=(inside,) * 3,
         scratch_shapes=[
             vm((4, 512, 256), BF), vm((4, 512, 512), BF), vm((4, 512, 256), BF),
             vm((3, 512, 512), BF), vm((3, 512, 256), BF),
@@ -435,14 +453,21 @@
             vm((2, 64, 256), BF), vm((2, 64, 256), BF), vm((8, 64, 256), BF), vm((8, 64, 256), BF),
             vm((2, 64, 256), BF), vm((2, 64, 256), BF), vm((2, 128, 256), BF), vm((128, 256), BF),
             vm((2, 128, 256), BF), vm((2, 128, 256), BF), vm((256, 256), BF), vm((256, 256), BF),
-            vm((4, 512, 256), F32), vm((4, 512, 256), BF),
-            dma((5, 4)), dma((9,)), dma((4,)), dma((7,)), dma((92,)), dma((9,)), dma((15,)),
+            dma((5, 4)), dma((9,)), dma((7,)), dma((61,)), dma((11,)), dma((15,)),
             dma((4, 4)), dma((5, 16)), dma((13,)), dma((8,)), dma((8,)),
         ],
         compiler_params=pltpu.CompilerParams(
-            collective_id=0, has_side_effects=True, vmem_limit_bytes=56 << 20
+            collective_id=0, has_side_effects=True, vmem_limit_bytes=24 << 20
         ),
     )(*flat)
+    out = pl.pallas_call(
+        final_kernel,
+        out_shape=jax.ShapeDtypeStruct((2048, 256), F32),
+        in_specs=[inside] * 3,
+        out_specs=pl.BlockSpec(memory_space=pl.ANY),
+        scratch_shapes=[vm((8, 256, 256), F32), dma((8,))],
+        compiler_params=pltpu.CompilerParams(vmem_limit_bytes=16 << 20),
+    )(*parts)
     return out.reshape(1, 2048, 256)
 
 

time: 56.6 us -> 53.4 us (0.943)
  local copies, waits for them, and re-layouts: 3.05 us -> 0 us
    unnamed x1 -> x0, local copies, waits for them, and re-layouts: 3.05 us -> none
    pallas_call x1 -> x2, Pallas kernels: 53.5 us -> 53.4 us  [the longest x1 50.8 us: body(): pl.pallas_call(kernel, out_shape=(jax.ShapeDtypeStruct((4, 512, 256), F32...]
where the time goes in v3:
time: 53.4 us
  Pallas kernels  53.4 us (100%)
    pallas_call x1, Pallas kernels, body(): pl.pallas_call(kernel, out_shape=(jax.ShapeDtypeStruct((4, 512, 256), F32...  50.8 us
    pallas_call x1, Pallas kernels, body(): pl.pallas_call(final_kernel, out_shape=jax.ShapeDtypeStruct((2048, 256),...  2.57 us

profile of v3, /device:TPU:1, one launch (start us, length us, event | category | flops | bytes accessed | tf_op | source)
XLA Modules:
  0.0 53.4 jit_solution(17626591162434601077)
XLA Ops:
  0.0 50.8 %shard_map.82 = (f32[4,512,256]{2,1,0:T(8,128)S(1)}, bf16[4,512,256]{2,1,0:T(8,128)(2,1)S(1)}, bf16[256,256]{1,0:T(8,128)(2,1)S(1)}) custom-call(bf16[2048,256]{1,0:T(8,128)(2,1)} %bitcast.10, bf16[2048,512]{1,0:T(8,128)(2,1)} %bitcast.8, bf16[2048,256]{1,0:T(8,128)(2,1)} %bitcast.11, bf16[1536,512]{1,0:T(8,128)(2,1)} %bitcast.9, ...), custom_call_target="tpu_custom_call" | custom-call | tf_op jit(solution)/shard_map/pallas_call | solution.py:437
  50.8 2.6 %shard_map.83 = f32[2048,256]{1,0:T(8,128)} custom-call(f32[4,512,256]{2,1,0:T(8,128)S(1)} %get-tuple-element.8.sv, bf16[4,512,256]{2,1,0:T(8,128)(2,1)S(1)} %get-tuple-element.9.hv, bf16[256,256]{1,0:T(8,128)(2,1)S(1)} %get-tuple-element.10.top), custom_call_target="tpu_custom_call" | custom-call | tf_op jit(solution)/shard_map/pallas_call | solution.py:463

commit v4 on v3

--- a/solution.py
+++ b/solution.py
@@ -179,9 +179,11 @@
         return V(rings[a][1])[i], V(ring_sem)[a, i]
 
     def ring_own(which, arrays, to):
+        started = []
         for a in arrays:
             dst, sem = spot(a, "own")
-            send(which, rings[a][0], dst, sem, (to, r))
+            started.append(send(which, rings[a][0], dst, sem, (to, r)))
+        return started
 
     def relay(name, arrays, *to):
         for a in arrays:
@@ -195,12 +197,10 @@
         ring_own(1, (0, 1), mate)
         send(1, V(um_hbm)[second], V(m2)[to_proc2], V(up_sem)[0, 2], (mate, r))
         send(1, V(uw_hbm)[second], V(w2)[to_proc2], V(up_sem)[1, 2], (mate, r))
-        ring_own(1, (2, 3), far)
 
     @pl.when(is_proc == 1)
     def _():
         ring_own(0, (0, 1, 2, 3), mate)
-        ring_own(0, (2, 3), cross)
 
     send(2, V(um_hbm)[first], V(m1)[place1], V(up_sem)[2, 0], (partner, r))
     send(2, V(uw_hbm)[first], V(w1)[place1], V(up_sem)[3, 0], (partner, r))
@@ -210,7 +210,6 @@
         send(0, V(um_hbm)[second], V(m2)[here2], V(up_sem)[0, 1], (partner, r))
         send(0, V(uw_hbm)[second], V(w2)[here2], V(up_sem)[1, 1], (partner, r))
         ring_own(0, (0, 1, 2, 3, 4), partner)
-        ring_own(0, (4,), mate)
 
     def leaf_up(i, carry):
         for c in load(i):
@@ -268,7 +267,9 @@
     def _():
         first_sent = send(1, c1, V(p2)[side_no], V(small_sem)[1], (mate, r))
         flush(1, [first_sent])
-        ring_own(1, (2, 3, 4), mate)
+        fourth_sent = ring_own(1, (2, 3), mate) + ring_own(1, (2, 3), far)
+        flush(1, fourth_sent)
+        ring_own(1, (4,), mate)
         arrived(kr, small_sem.at[10])
         own_gain(kr[...])
         arrived(f1, small_sem.at[11])
@@ -277,14 +278,13 @@
     def _():
         p2[child] = c1[...]
         relay("edge", (0, 1), mate, partner)
+        ring_own(0, (2, 3), cross)
         arrived(m2.at[part2(edge2)], up_sem.at[0, 2])
         send(0, V(m2)[edge_rows2], V(m2)[edge_rows2], V(up_sem)[0, 3], (partner, r))
         arrived(w2.at[part2(edge2)], up_sem.at[1, 2])
         send(0, V(w2)[edge_rows2], V(w2)[edge_rows2], V(up_sem)[1, 3], (partner, r))
         relay("mate", (0, 1), partner)
         relay("mate", (2, 3), partner)
-        relay("x_own", (2, 3), mate, partner)
-        relay("x_edge", (2, 3), mate, partner)
         for i, c in ((1, beside2), (3, beside_edge2)):
             arrived(m2.at[part2(c)], up_sem.at[0, i])
             arrived(w2.at[part2(c)], up_sem.at[1, i])
@@ -297,17 +297,20 @@
             for i in range(4):
                 j = lax.rem(partner + 2 * i, 8)
                 arrived(rings[a][1].at[j], ring_sem.at[a, j])
+        relay("edge", (2, 3), mate, partner)
+        relay("x_own", (2, 3), mate, partner)
+        relay("x_edge", (2, 3), mate, partner)
         arrived(p3.at[1 - side_no], small_sem.at[2])
         m3 = rm[...].reshape(512, 512)
         w3 = rw[...].reshape(512, 256)
         pair3 = side(p3, 0)
         p4[n] = node_up(pair3, m3, w3)
         send(0, V(p4)[n], V(p4)[n], V(small_sem)[3], (opposite, r))
+        ring_own(0, (4,), mate)
+        relay("mate_edge", (2, 3), partner)
         relay("x_mate", (2, 3), partner)
         relay("x_mate_edge", (2, 3), partner)
-        relay("edge", (2, 3), mate, partner)
         relay("edge", (4,), mate, partner)
-        relay("mate_edge", (2, 3), partner)
         for a in (2, 3):
             for i in range(8):
                 j = lax.rem(partner + 2 * i, 16)
@@ -329,9 +332,6 @@
         t2s[1] = t2[:, 256:]
         send(0, V(t2s)[child], V(f2)[side_no], V(small_sem)[6], (mate, r))
         f2[side_no] = t2s[side_no]
-        relay("mate", (4,), partner)
-        relay("mate_edge", (4,), partner)
-
         m4h = xm[pl.ds(base, 8)].reshape(256, 512)
         e = mul(m4h, w4).astype(BF)
         m3h = rm[pl.ds(4 * side_no, 4)].reshape(256, 512)
@@ -342,6 +342,8 @@
         send(0, ks, kr, V(small_sem)[10], (edge, r))
         m2_own = m2[pl.ds(pl.multiple_of(256 * child, 256), 256), :]
         own_gain(mul(m2_own, lifted2).astype(BF))
+        relay("mate", (4,), partner)
+        relay("mate_edge", (4,), partner)
         arrived(f2.at[child], small_sem.at[6])
         t1 = node_down(side(p2, 0), f2[...].reshape(128, 256), m2[...], w2[...])
         t1s[0] = t1[:, :256]

time: 53.4 us -> 52.1 us (0.976)
  Pallas kernels: 53.4 us -> 52 us
    pallas_call x1, Pallas kernels: 50.8 us -> 49.4 us  [body(): pl.pallas_call(kernel, out_shape=(jax.ShapeDtypeStruct((4, 512, 256), F32...]
where the time goes in v4:
time: 52.1 us; the launch traced here: 52 us
  Pallas kernels  52 us (100%)
    pallas_call x1, Pallas kernels, body(): pl.pallas_call(kernel, out_shape=(jax.ShapeDtypeStruct((4, 512, 256), F32...  49.4 us
    pallas_call x1, Pallas kernels, body(): pl.pallas_call(final_kernel, out_shape=jax.ShapeDtypeStruct((2048, 256),...  2.57 us

profile of v4, /device:TPU:1, one launch (start us, length us, event | category | flops | bytes accessed | tf_op | source)
XLA Modules:
  0.0 52.0 jit_solution(5339891482647123425)
XLA Ops:
  0.0 49.4 %shard_map.82 = (f32[4,512,256]{2,1,0:T(8,128)S(1)}, bf16[4,512,256]{2,1,0:T(8,128)(2,1)S(1)}, bf16[256,256]{1,0:T(8,128)(2,1)S(1)}) custom-call(bf16[2048,256]{1,0:T(8,128)(2,1)} %bitcast.10, bf16[2048,512]{1,0:T(8,128)(2,1)} %bitcast.8, bf16[2048,256]{1,0:T(8,128)(2,1)} %bitcast.11, bf16[1536,512]{1,0:T(8,128)(2,1)} %bitcast.9, ...), custom_call_target="tpu_custom_call" | custom-call | tf_op jit(solution)/shard_map/pallas_call | solution.py:439
  49.4 2.6 %shard_map.83 = f32[2048,256]{1,0:T(8,128)} custom-call(f32[4,512,256]{2,1,0:T(8,128)S(1)} %get-tuple-element.8.sv, bf16[4,512,256]{2,1,0:T(8,128)(2,1)S(1)} %get-tuple-element.9.hv, bf16[256,256]{1,0:T(8,128)(2,1)S(1)} %get-tuple-element.10.top), custom_call_target="tpu_custom_call" | custom-call | tf_op jit(solution)/shard_map/pallas_call | solution.py:465
